TPU v7x, 256 devices: a whole 4x4x8 slice. The times are simulated.
256 devices in a mesh: segment: 4 (over y), frame: 16 (over z, core), row: 4 (over x).
Axes of the slice: x: 4, y: 4, z: 8, core: 2. Of those that a mesh axis runs over, the one named last changes fastest.
Arguments:
- latents: bfloat16 [2, 32, 8, 24, 320], P(None, 'frame', 'row')
- cotangent: bfloat16 [2, 32, 8, 24, 320], P(None, 'frame', 'row'), may hold values from -0.0546875 to 0.0546875
- timesteps: int32 [2], replicated, may hold values from 0 to 999
- frame_counts: int32 [2], replicated, may hold values from 8 to 32, as said below
- spatial_weight: bfloat16 [4, 9, 320, 320], P('segment'), may hold values from -0.109375 to 0.109375
- temporal_weight: bfloat16 [4, 3, 320, 320], P('segment'), may hold values from -0.1875 to 0.1875
- time_weight: bfloat16 [4, 1280, 320], P('segment'), may hold values from -0.15625 to 0.15625
- norm_gain: float32 [4, 320], P('segment'), may hold values from 0.5 to 1.5
Outputs:
- spatial_grad: float32 [4, 2880, 320], P('segment', ('frame', 'row'))
- temporal_grad: float32 [4, 960, 320], P('segment', ('frame', 'row'))
- time_grad: float32 [4, 1280, 320], P('segment', ('frame', 'row'))
- gain_grad: float32 [4, 320], P('segment', ('frame', 'row'))
Inputs may be any that keep to these rules, and one draw needn't show every extreme that they name: Frames frame_counts[c] and later of clip c are padding; some clip has all 32 frames.
All inputs are finite; a program needn't handle non-finite values.
Results may differ from a plain program's by a relative error of at most 0.02.
Values may be sent and summed in bfloat16 or wider, within the bound.
No kernel may reach another device: no remote copies, remote signals or barrier semaphores. Data moves between devices by JAX's collectives and lax.ppermute only.
A program may use at most 128 MiB of HBM per device.

v0:
```python
import jax
import jax.numpy as jnp
from jax import lax
from jax.sharding import PartitionSpec as P

C = 320
G = 32
TE = 1280
WIDTH = 24
R_DEV = 2
F_DEV = 2
CLIPS = 2
EPSILON = 1e-05


def with_halo(array, sides, width):
    for axis, dim in sides:
        peers, length = (lax.axis_size(axis), array.shape[dim])
        up = [(i, (i + 1) % peers) for i in range(peers - 1)]
        down = [(j, i) for i, j in up]
        last = lax.slice_in_dim(array, length - width, length, axis=dim)
        leading = lax.slice_in_dim(array, 0, width, axis=dim)
        before = lax.ppermute(last, axis, up)
        after = lax.ppermute(leading, axis, down)
        array = jnp.concatenate([before, array, after], axis=dim)
    return array


def shifted(array, axis, by):
    peers = lax.axis_size(axis)
    pairs = [(i, i + by) for i in range(peers) if 0 <= i + by < peers]
    return lax.ppermute(array, axis, pairs)


def time_features(timesteps):
    half_dim = TE // 2
    frequency = jnp.exp(-jnp.log(10000.0) * jnp.arange(half_dim).astype(jnp.float32) / half_dim)
    angles = timesteps.astype(jnp.float32)[:, None] * frequency[None, :]
    wave_parts = jnp.concatenate([jnp.cos(angles), jnp.sin(angles)], axis=1)
    return jax.nn.silu(wave_parts).astype(jnp.bfloat16)


def group_sum(values):
    per_channel = jnp.sum(values, axis=(0, 1, 2))
    return per_channel.reshape(G, -1).sum(axis=1)


def spread(values):
    return jnp.repeat(values, C // G)


def spatial_columns(padded, row_count, col_count):
    return jnp.concatenate(
        [
            padded[:, vertical : vertical + row_count, lateral : lateral + col_count, :]
            for vertical in range(3)
            for lateral in range(3)
        ],
        axis=-1,
    )


def flip_columns(padded, row_count, col_count):
    return jnp.concatenate(
        [
            padded[
                :, 2 - vertical : 2 - vertical + row_count, 2 - lateral : 2 - lateral + col_count, :
            ]
            for vertical in range(3)
            for lateral in range(3)
        ],
        axis=-1,
    )


def time_columns(padded, frame_count):
    return jnp.concatenate([padded[offset : offset + frame_count] for offset in range(3)], axis=-1)


def time_flip(padded, frame_count):
    return jnp.concatenate(
        [padded[2 - offset : 2 - offset + frame_count] for offset in range(3)], axis=-1
    )


def flat_dot(columns, matrix):
    return jnp.dot(columns.reshape(-1, matrix.shape[0]), matrix, preferred_element_type=jnp.float32)


def outer_dot(columns, right_side):
    return lax.dot_general(
        columns.reshape(-1, columns.shape[-1]),
        right_side.reshape(-1, right_side.shape[-1]),
        (((0,), (0,)), ((), ())),
        preferred_element_type=jnp.float32,
    )


def remember(store, value, clip_index, is_live):
    old_value = lax.dynamic_index_in_dim(store, clip_index, 0, keepdims=False)
    return lax.dynamic_update_index_in_dim(
        store, jnp.where(is_live, value, old_value), clip_index, 0
    )


def pick_row(table, clip_index):
    return lax.dynamic_index_in_dim(table, clip_index, 0, keepdims=False)


def per_device(
    latents,
    cotangent,
    timesteps,
    frame_counts,
    spatial_weight,
    temporal_weight,
    time_weight,
    norm_gain,
):
    sections = lax.axis_size("segment")
    segment_index = lax.axis_index("segment")
    all_rows = R_DEV * lax.axis_size("row")
    group_width = C // G
    tick_total = CLIPS + sections - 1
    act_shape = (F_DEV, R_DEV, WIDTH, C)
    kernel = spatial_weight[0]
    tkernel = temporal_weight[0]
    gain_row = norm_gain[0]
    kernel_flat = kernel.reshape(9 * C, C)
    kernel_back = jnp.transpose(kernel, (0, 2, 1)).reshape(9 * C, C)
    tkernel_flat = tkernel.reshape(3 * C, C)
    tkernel_back = jnp.transpose(tkernel, (0, 2, 1)).reshape(3 * C, C)
    time_embed = time_features(timesteps)
    clip_biases = jnp.dot(time_embed, time_weight[0], preferred_element_type=jnp.float32)
    frame_ids = lax.axis_index("frame") * F_DEV + jnp.arange(F_DEV)
    zero_act = jnp.zeros(act_shape, jnp.bfloat16)

    def frame_mask_of(clip_index):
        frame_limit = pick_row(frame_counts, clip_index)
        frame_mask = (frame_ids < frame_limit).astype(jnp.float32)[:, None, None, None]
        cell_total = frame_limit.astype(jnp.float32) * all_rows * WIDTH * group_width
        return (frame_mask, cell_total)

    padded_in_store = jnp.zeros((CLIPS, F_DEV, R_DEV + 2, WIDTH + 2, C), jnp.bfloat16)
    hidden_store = jnp.zeros((CLIPS,) + act_shape, jnp.float32)
    padded_act_store = jnp.zeros((CLIPS, F_DEV + 2, R_DEV, WIDTH, C), jnp.bfloat16)
    mean_store = jnp.zeros((CLIPS, G), jnp.float32)
    inverse_store = jnp.zeros((CLIPS, G), jnp.float32)
    received = zero_act
    skip_queue = []
    for tick_step in range(tick_total):
        clip_raw = tick_step - segment_index
        is_live = (clip_raw >= 0) & (clip_raw < CLIPS)
        clip_index = jnp.clip(clip_raw, 0, CLIPS - 1)
        first_input = latents[min(tick_step, CLIPS - 1)]
        current = jnp.where(segment_index == 0, first_input, received)
        arriving = skip_queue[tick_step - sections + 1] if tick_step >= sections - 1 else zero_act
        joined = (current.astype(jnp.float32) + arriving.astype(jnp.float32)).astype(jnp.bfloat16)
        current = jnp.where(segment_index == sections - 1, joined, current)
        frame_mask, cell_total = frame_mask_of(clip_index)
        padded_rows = with_halo(current, (("row", 1),), 1)
        padded_in = jnp.pad(padded_rows, ((0, 0), (0, 0), (1, 1), (0, 0)))
        hidden = flat_dot(spatial_columns(padded_in, R_DEV, WIDTH), kernel_flat).reshape(
            act_shape
        ) + pick_row(clip_biases, clip_index)
        masked = hidden * frame_mask
        group_mean = lax.psum(group_sum(masked), ("frame", "row")) / cell_total
        centred = hidden - spread(group_mean)
        variance = (
            lax.psum(group_sum(frame_mask * centred * centred), ("frame", "row")) / cell_total
        )
        inv_spread = lax.rsqrt(variance + EPSILON)
        normed = centred * spread(inv_spread)
        activated = (frame_mask * jax.nn.silu(normed * gain_row)).astype(jnp.bfloat16)
        padded_act = with_halo(activated, (("frame", 0),), 1)
        temporal = flat_dot(time_columns(padded_act, F_DEV), tkernel_flat).reshape(act_shape)
        output = (current.astype(jnp.float32) + temporal).astype(jnp.bfloat16)
        padded_in_store = remember(padded_in_store, padded_in, clip_index, is_live)
        hidden_store = remember(hidden_store, hidden, clip_index, is_live)
        padded_act_store = remember(padded_act_store, padded_act, clip_index, is_live)
        mean_store = remember(mean_store, group_mean, clip_index, is_live)
        inverse_store = remember(inverse_store, inv_spread, clip_index, is_live)
        received = shifted(output, "segment", 1)
        skip_queue.append(shifted(output, "segment", sections - 1))
    spatial_acc = jnp.zeros((9 * C, C), jnp.float32)
    temporal_acc = jnp.zeros((3 * C, C), jnp.float32)
    gain_acc = jnp.zeros((C,), jnp.float32)
    time_acc = jnp.zeros((TE, C), jnp.float32)
    upstream_recv = zero_act
    grad_queue = []
    for tick_step in range(tick_total):
        clip_raw = tick_step - (sections - 1 - segment_index)
        is_live = (clip_raw >= 0) & (clip_raw < CLIPS)
        clip_index = jnp.clip(clip_raw, 0, CLIPS - 1)
        frame_mask, cell_total = frame_mask_of(clip_index)
        last_grad = (frame_mask * pick_row(cotangent, clip_index).astype(jnp.float32)).astype(
            jnp.bfloat16
        )
        upstream = jnp.where(segment_index == sections - 1, last_grad, upstream_recv)
        arriving = grad_queue[tick_step - sections + 1] if tick_step >= sections - 1 else zero_act
        joined = (upstream.astype(jnp.float32) + arriving.astype(jnp.float32)).astype(jnp.bfloat16)
        upstream = jnp.where(segment_index == 0, joined, upstream)
        padded_in = pick_row(padded_in_store, clip_index)
        hidden = pick_row(hidden_store, clip_index)
        padded_act = pick_row(padded_act_store, clip_index)
        group_mean = pick_row(mean_store, clip_index)
        inv_spread = pick_row(inverse_store, clip_index)
        padded_up = with_halo(upstream, (("frame", 0),), 1)
        act_grad = flat_dot(time_flip(padded_up, F_DEV), tkernel_back).reshape(act_shape)
        temporal_part = outer_dot(time_columns(padded_act, F_DEV), upstream)
        normed = (hidden - spread(group_mean)) * spread(inv_spread)
        scaled = normed * gain_row
        gate_sig = jax.nn.sigmoid(scaled)
        scaled_grad = act_grad * frame_mask * gate_sig * (1.0 + scaled * (1.0 - gate_sig))
        gain_part = jnp.sum(scaled_grad * normed, axis=(0, 1, 2))
        normed_grad = scaled_grad * gain_row
        first_total, second_total = lax.psum(
            (group_sum(normed_grad), group_sum(normed_grad * normed)), ("frame", "row")
        )
        first_moment = first_total / cell_total
        second_moment = second_total / cell_total
        hidden_grad = (
            spread(inv_spread)
            * (normed_grad - frame_mask * (spread(first_moment) + normed * spread(second_moment)))
        ).astype(jnp.bfloat16)
        column_sums = jnp.sum(hidden_grad.astype(jnp.float32), axis=(0, 1, 2))
        spatial_part = outer_dot(spatial_columns(padded_in, R_DEV, WIDTH), hidden_grad)
        padded_grad = with_halo(hidden_grad, (("row", 1),), 1)
        padded_grad = jnp.pad(padded_grad, ((0, 0), (0, 0), (1, 1), (0, 0)))
        conv_back = flat_dot(flip_columns(padded_grad, R_DEV, WIDTH), kernel_back).reshape(
            act_shape
        )
        input_grad = (upstream.astype(jnp.float32) + conv_back).astype(jnp.bfloat16)
        spatial_acc = spatial_acc + jnp.where(is_live, spatial_part, 0.0)
        temporal_acc = temporal_acc + jnp.where(is_live, temporal_part, 0.0)
        gain_acc = gain_acc + jnp.where(is_live, gain_part, 0.0)
        embed_row = pick_row(time_embed, clip_index).astype(jnp.float32)
        time_acc = time_acc + jnp.where(is_live, embed_row[:, None] * column_sums[None, :], 0.0)
        upstream_recv = shifted(input_grad, "segment", -1)
        grad_queue.append(shifted(input_grad, "segment", -(sections - 1)))
    spatial_out, temporal_out, time_out, gain_out = (
        lax.psum_scatter(spatial_acc, ("frame", "row"), scatter_dimension=0, tiled=True),
        lax.psum_scatter(temporal_acc, ("frame", "row"), scatter_dimension=0, tiled=True),
        lax.psum_scatter(time_acc, ("frame", "row"), scatter_dimension=0, tiled=True),
        lax.psum_scatter(gain_acc, ("frame", "row"), scatter_dimension=0, tiled=True),
    )
    return (spatial_out[None], temporal_out[None], time_out[None], gain_out[None])


def solution(mesh):
    return jax.shard_map(
        per_device,
        mesh=mesh,
        in_specs=(
            P(None, "frame", "row", None, None),
            P(None, "frame", "row", None, None),
            P(),
            P(),
            P("segment", None, None, None),
            P("segment", None, None, None),
            P("segment", None, None),
            P("segment", None),
        ),
        out_specs=(
            P("segment", ("frame", "row"), None),
            P("segment", ("frame", "row"), None),
            P("segment", ("frame", "row"), None),
            P("segment", ("frame", "row")),
        ),
        check_vma=False,
    )
```

profile of v0, /device:TPU:80, one launch (start us, length us, event | category | flops | bytes accessed | tf_op | source)
XLA Modules:
  0.0 2447.7 jit_solution(5756739828602763937)
XLA Ops:
  9.6 4.5 collective-permute-start
  20.2 3.6 collective-permute-start.24
  53.3 106.2 %psum.140 = f32[32]{0:T(128)S(1)} all-reduce(f32[32]{0:T(128)S(1)} %reduce_sum.451), channel_id=1, replica_groups=mesh['segment'=4,'frame'=16,'row'=4] {'frame','row'}, use_global_device_ids=true, to_apply=%region_2.3 | all-reduce | flops 32 | bytes 256 | tf_op jit(solution)/shard_map/psum | solution.py:167
  160.5 124.5 %psum.141 = f32[32]{0:T(128)S(1)} all-reduce(f32[32]{0:T(128)S(1)} %reduce_sum.453), channel_id=1, replica_groups=mesh['segment'=4,'frame'=16,'row'=4] {'frame','row'}, use_global_device_ids=true, to_apply=%region_5.6 | all-reduce | flops 32 | bytes 256 | tf_op jit(solution)/shard_map/psum | solution.py:170
  286.7 7.3 collective-permute-start.3
  298.9 3.5 collective-permute-done.2
  304.6 3.3 collective-permute-start.4
  312.5 4.8 collective-permute-start.5
  324.2 118.3 %psum.142 = f32[32]{0:T(128)S(1)} all-reduce(f32[32]{0:T(128)S(1)} %reduce_sum.455), channel_id=1, replica_groups=mesh['segment'=4,'frame'=16,'row'=4] {'frame','row'}, use_global_device_ids=true, to_apply=%region_8.9 | all-reduce | flops 32 | bytes 256 | tf_op jit(solution)/shard_map/psum | solution.py:167
  443.5 125.7 %psum.143 = f32[32]{0:T(128)S(1)} all-reduce(f32[32]{0:T(128)S(1)} %reduce_sum.457), channel_id=1, replica_groups=mesh['segment'=4,'frame'=16,'row'=4] {'frame','row'}, use_global_device_ids=true, to_apply=%region_11.12 | all-reduce | flops 32 | bytes 256 | tf_op jit(solution)/shard_map/psum | solution.py:170
  571.3 5.4 collective-permute-start.8
  587.1 3.2 collective-permute-start.9
  594.7 4.8 collective-permute-start.10
  606.5 119.5 %psum.144 = f32[32]{0:T(128)S(1)} all-reduce(f32[32]{0:T(128)S(1)} %reduce_sum.459), channel_id=1, replica_groups=mesh['segment'=4,'frame'=16,'row'=4] {'frame','row'}, use_global_device_ids=true, to_apply=%region_14.15 | all-reduce | flops 32 | bytes 256 | tf_op jit(solution)/shard_map/psum | solution.py:167
  727.0 125.7 %psum.145 = f32[32]{0:T(128)S(1)} all-reduce(f32[32]{0:T(128)S(1)} %reduce_sum.461), channel_id=1, replica_groups=mesh['segment'=4,'frame'=16,'row'=4] {'frame','row'}, use_global_device_ids=true, to_apply=%region_17.18 | all-reduce | flops 32 | bytes 256 | tf_op jit(solution)/shard_map/psum | solution.py:170
  854.0 5.6 collective-permute-start.13
  859.6 2.9 collective-permute-start.12
  869.6 3.2 collective-permute-start.14
  878.1 4.8 collective-permute-start.16
  891.2 119.9 %psum.146 = f32[32]{0:T(128)S(1)} all-reduce(f32[32]{0:T(128)S(1)} %reduce_sum.463), channel_id=1, replica_groups=mesh['segment'=4,'frame'=16,'row'=4] {'frame','row'}, use_global_device_ids=true, to_apply=%region_20.21 | all-reduce | flops 32 | bytes 256 | tf_op jit(solution)/shard_map/psum | solution.py:167
  1015.3 125.6 %psum.147 = f32[32]{0:T(128)S(1)} all-reduce(f32[32]{0:T(128)} %reduce_sum.465), channel_id=1, replica_groups=mesh['segment'=4,'frame'=16,'row'=4] {'frame','row'}, use_global_device_ids=true, to_apply=%region_23.24 | all-reduce | flops 32 | bytes 256 | tf_op jit(solution)/shard_map/psum | solution.py:170
  1143.2 5.3 collective-permute-start.19
  1148.5 2.9 collective-permute-start.18
  1152.3 4.7 collective-permute-done.18
  1158.5 3.2 collective-permute-start.20
  1161.7 3.5 collective-permute-done.20
  1168.1 4.8 collective-permute-start.22
  1180.6 119.4 %psum.148 = f32[32]{0:T(128)S(1)} all-reduce(f32[32]{0:T(128)S(1)} %reduce_sum.467), channel_id=1, replica_groups=mesh['segment'=4,'frame'=16,'row'=4] {'frame','row'}, use_global_device_ids=true, to_apply=%region_26.27 | all-reduce | flops 32 | bytes 256 | tf_op jit(solution)/shard_map/psum | solution.py:167
  1301.4 125.7 %psum.149 = f32[32]{0:T(128)S(1)} all-reduce(f32[32]{0:T(128)S(1)} %reduce_sum.469), channel_id=1, replica_groups=mesh['segment'=4,'frame'=16,'row'=4] {'frame','row'}, use_global_device_ids=true, to_apply=%region_29.30 | all-reduce | flops 32 | bytes 256 | tf_op jit(solution)/shard_map/psum | solution.py:170
  1429.6 2.7 multiply_reduce_fusion.4
  1432.8 124.9 %all-reduce.19 = (f32[32]{0:T(128)S(1)}, f32[32]{0:T(128)S(1)}) all-reduce(f32[32]{0:T(128)S(1)} %reduce_sum.473, f32[32]{0:T(128)S(1)} %reduce_sum.471), channel_id=1, replica_groups=mesh['segment'=4,'frame'=16,'row'=4] {'frame','row'}, use_global_device_ids=true, to_apply=%region_35.36 | all-reduce | flops 64 | bytes 512 | tf_op jit(solution)/shard_map/psum | solution.py:217
  1561.0 4.5 collective-permute-start.26
  1572.3 3.9 collective-permute-start.28
  1579.3 4.2 collective-permute-start.30
  1587.3 9.5 collective-permute-done.29
  1596.7 2.7 multiply_reduce_fusion.3
  1599.9 118.5 %all-reduce.18 = (f32[32]{0:T(128)S(1)}, f32[32]{0:T(128)S(1)}) all-reduce(f32[32]{0:T(128)S(1)} %reduce_sum.477, f32[32]{0:T(128)S(1)} %reduce_sum.475), channel_id=1, replica_groups=mesh['segment'=4,'frame'=16,'row'=4] {'frame','row'}, use_global_device_ids=true, to_apply=%region_41.42 | all-reduce | flops 64 | bytes 512 | tf_op jit(solution)/shard_map/psum | solution.py:217
  1721.7 4.5 collective-permute-start.31
  1733.7 4.0 collective-permute-start.33
  1741.1 4.2 collective-permute-start.35
  1748.5 10.0 collective-permute-done.34
  1758.5 2.8 multiply_reduce_fusion.2
  1761.7 118.0 %all-reduce.17 = (f32[32]{0:T(128)S(1)}, f32[32]{0:T(128)S(1)}) all-reduce(f32[32]{0:T(128)S(1)} %reduce_sum.481, f32[32]{0:T(128)S(1)} %reduce_sum.479), channel_id=1, replica_groups=mesh['segment'=4,'frame'=16,'row'=4] {'frame','row'}, use_global_device_ids=true, to_apply=%region_47.48 | all-reduce | flops 64 | bytes 512 | tf_op jit(solution)/shard_map/psum | solution.py:217
  1882.5 4.5 collective-permute-start.36
  1894.7 4.0 collective-permute-start.38
  1904.0 4.7 collective-permute-start.41
  1927.7 125.8 %all-reduce.16 = (f32[32]{0:T(128)S(1)}, f32[32]{0:T(128)S(1)}) all-reduce(f32[32]{0:T(128)S(1)} %reduce_sum.485, f32[32]{0:T(128)S(1)} %reduce_sum.483), channel_id=1, replica_groups=mesh['segment'=4,'frame'=16,'row'=4] {'frame','row'}, use_global_device_ids=true, to_apply=%region_53.54 | all-reduce | flops 64 | bytes 512 | tf_op jit(solution)/shard_map/psum | solution.py:217
  2055.4 4.8 collective-permute-start.42
  2060.2 3.8 convolution_bitcast_fusion.3
  2072.5 2.9 convolution_bitcast_fusion.2
  2077.2 4.7 collective-permute-start.47
  2084.0 2.9 convolution_bitcast_fusion.1
  2087.0 7.7 collective-permute-done.46
  2095.6 117.5 %all-reduce.15 = (f32[32]{0:T(128)S(1)}, f32[32]{0:T(128)S(1)}, f32[320]{0:T(512)S(1)}) all-reduce(f32[32]{0:T(128)S(1)} %reduce_sum.489, f32[32]{0:T(128)S(1)} %reduce_sum.487, f32[320]{0:T(512)S(1)} %select_add_fusion.2), channel_id=1, replica_groups=mesh['segment'=4,'frame'=16,'row'=4] {'frame','row'}, use_global_device_ids=true, to_apply=%region_59.60 | all-reduce | flops 384 | bytes 3072 | tf_op jit(solution)/shard_map/psum | solution.py:217
  2215.6 6.3 collective-permute-start.48
  2226.9 7.5 select_add_fusion
  2237.6 153.2 %fusion.209 = (f32[48,320]{1,0:T(8,128)S(1)}, f32[16,320]{1,0:T(8,128)S(1)}) fusion(f32[2880,320]{1,0:T(8,128)} %select_add_fusion, f32[960,320]{1,0:T(8,128)S(1)} %fusion.2), kind=kCustom, calls=%all-reduce-scatter.2 | all-reduce-scatter fusion | flops 1310722 | bytes 4998144
  2390.8 5.3 collective-permute-start.56
  2396.1 5.4 collective-permute-start.55
  2401.5 3.5 collective-permute-start.54
  2405.0 8.1 collective-permute-start.57
  2413.7 7.1 collective-permute-start.52
  2420.8 4.7 collective-permute-start.51
  2425.5 6.8 collective-permute-start.50
  (584 shorter events, 224.4 us)
Async XLA Ops:
  7.2 2432.2 %all-reduce.23.cloned.1.call-start = ((), (), s32[]{:S(2)}) async-start(), calls=%async_computation | async-start | bytes 3932160
  8.3 42.3 %collective-permute-start.1 = (bf16[2,1,24,320]{3,2,1,0:T(8,128)(2,1)S(1)}, bf16[2,1,24,320]{3,2,1,0:T(8,128)(2,1)S(1)}, u32[]{:S(2)}, u32[]{:S(2)}) collective-permute-start(bf16[2,1,24,320]{3,2,1,0:T(8,128)(2,1)S(1)} %get-tuple-element.260), channel_id=1, source_target_pairs={{1,0},{2,1},{3,2},{5,4},{6,5},{7,6},{9,8},{10,9},{11,10},{13,12},{... | collective-permute-start | bytes 92168 | tf_op jit(solution)/shard_map/ppermute | solution.py:24
  9.6 41.0 %collective-permute-start = (bf16[2,1,24,320]{3,2,1,0:T(8,128)(2,1)S(1)}, bf16[2,1,24,320]{3,2,1,0:T(8,128)(2,1)S(1)}, u32[]{:S(2)}, u32[]{:S(2)}) collective-permute-start(bf16[2,1,24,320]{3,2,1,0:T(8,128)(2,1)S(1)} %get-tuple-element.259), channel_id=1, source_target_pairs={{0,1},{1,2},{2,3},{4,5},{5,6},{6,7},{8,9},{9,10},{10,11},{12,13},{... | collective-permute-start | bytes 92168 | tf_op jit(solution)/shard_map/ppermute | solution.py:23
  18.3 1411.3 %collective-permute-start.25 = (bf16[1,2,24,320]{3,2,1,0:T(8,128)(2,1)}, bf16[1,2,24,320]{3,2,1,0:T(8,128)(2,1)}, u32[]{:S(2)}, u32[]{:S(2)}) collective-permute-start(bf16[1,2,24,320]{3,2,1,0:T(8,128)(2,1)} %get-tuple-element.234), channel_id=1, source_target_pairs={{0,4},{4,8},{8,12},{12,16},{16,20},{20,24},{24,28},{28,32},{32,36}... | collective-permute-start | bytes 92168 | tf_op jit(solution)/shard_map/ppermute | solution.py:23
  20.2 1409.4 %collective-permute-start.24 = (bf16[1,2,24,320]{3,2,1,0:T(8,128)(2,1)}, bf16[1,2,24,320]{3,2,1,0:T(8,128)(2,1)}, u32[]{:S(2)}, u32[]{:S(2)}) collective-permute-start(bf16[1,2,24,320]{3,2,1,0:T(8,128)(2,1)} %get-tuple-element.233), channel_id=1, source_target_pairs={{4,0},{8,4},{12,8},{16,12},{20,16},{24,20},{28,24},{32,28},{36,32}... | collective-permute-start | bytes 92168 | tf_op jit(solution)/shard_map/ppermute | solution.py:24
  27.0 826.4 %copy-start.74 = (f32[2]{0:T(128)}, f32[2]{0:T(128)S(1)}, u32[]{:S(2)}) copy-start(f32[2]{0:T(128)S(1)} %compare_convert_fusion.7) | copy-start | bytes 28
  286.7 12.3 collective-permute-start.3
  293.9 8.6 collective-permute-start.2
  304.6 6.6 collective-permute-start.4
  308.6 565.0 %collective-permute-start.15 = (bf16[2,2,24,320]{3,2,1,0:T(8,128)(2,1)}, bf16[2,2,24,320]{3,2,1,0:T(8,128)(2,1)}, u32[]{:S(2)}, u32[]{:S(2)}) collective-permute-start(bf16[2,2,24,320]{3,2,1,0:T(8,128)(2,1)} %fusion.16), channel_id=1, source_target_pairs={{0,192},{1,193},{2,194},{3,195},{4,196},{5,197},{6,198},{7,199},{8... | collective-permute-start | bytes 184328 | tf_op jit(solution)/shard_map/ppermute | solution.py:32
  311.2 7.0 collective-permute-start.6
  312.5 6.4 collective-permute-start.5
  571.3 12.2 collective-permute-start.8
  576.7 8.9 collective-permute-start.7
  587.1 6.2 collective-permute-start.9
  593.4 7.0 collective-permute-start.11
  594.7 6.4 collective-permute-start.10
  854.0 11.9 collective-permute-start.13
  859.6 8.6 collective-permute-start.12
  865.8 295.9 %collective-permute-start.21 = (bf16[2,2,24,320]{3,2,1,0:T(8,128)(2,1)}, bf16[2,2,24,320]{3,2,1,0:T(8,128)(2,1)}, u32[]{:S(2)}, u32[]{:S(2)}) collective-permute-start(bf16[2,2,24,320]{3,2,1,0:T(8,128)(2,1)} %copy-done.98), channel_id=1, source_target_pairs={{0,192},{1,193},{2,194},{3,195},{4,196},{5,197},{6,198},{7,199},{8... | collective-permute-start | bytes 184328 | tf_op jit(solution)/shard_map/ppermute | solution.py:32
  869.6 6.2 collective-permute-start.14
  876.8 284.9 %copy-start.9 = (bf16[2,2,24,320]{3,2,1,0:T(8,128)(2,1)}, bf16[2,2,24,320]{3,2,1,0:T(8,128)(2,1)S(1)}, u32[]{:S(2)}) copy-start(bf16[2,2,24,320]{3,2,1,0:T(8,128)(2,1)S(1)} %fusion.136) | copy-start | bytes 184324
  876.8 6.9 collective-permute-start.17
  878.1 6.4 collective-permute-start.16
  888.0 263.4 %copy-start.42 = (bf16[1,2,2,24,320]{4,3,2,1,0:T(8,128)(2,1)S(1)}, bf16[1,2,2,24,320]{4,3,2,1,0:T(8,128)(2,1)}, u32[]{:S(2)}) copy-start(bf16[1,2,2,24,320]{4,3,2,1,0:T(8,128)(2,1)} %fusion.289) | copy-start | bytes 184324
  1143.2 9.1 collective-permute-start.19
  1148.5 8.6 collective-permute-start.18
  1158.5 6.8 collective-permute-start.20
  1166.8 7.6 collective-permute-start.23
  1168.1 6.4 collective-permute-start.22
  1178.0 251.6 %copy-start.27 = (bf16[2,2,24,320]{3,2,1,0:T(8,128)(2,1)S(1)}, bf16[2,2,24,320]{3,2,1,0:T(8,128)(2,1)}, u32[]{:S(2)}) copy-start(bf16[2,2,24,320]{3,2,1,0:T(8,128)(2,1)} %copy-done.26) | copy-start | bytes 184324
  1559.7 7.0 collective-permute-start.27
  1561.0 6.2 collective-permute-start.26
  1572.3 6.2 collective-permute-start.28
  1579.3 7.9 collective-permute-start.30
  1583.6 13.1 collective-permute-start.29
  1720.4 6.8 collective-permute-start.32
  1721.7 6.2 collective-permute-start.31
  1733.7 6.6 collective-permute-start.33
  1741.1 7.4 collective-permute-start.35
  1745.2 13.2 collective-permute-start.34
  1881.2 8.3 collective-permute-start.37
  1882.5 7.0 collective-permute-start.36
  1888.2 11.8 collective-permute-start.39
  1894.7 7.6 collective-permute-start.38
  1904.0 21.8 collective-permute-start.41
  1908.7 17.1 collective-permute-start.40
  2054.1 11.3 collective-permute-start.43
  2055.4 10.0 collective-permute-start.42
  2064.1 11.3 collective-permute-start.45
  2069.8 6.4 collective-permute-start.44
  2077.2 9.8 collective-permute-start.47
  2082.0 12.8 collective-permute-start.46
  2213.7 20.8 collective-permute-start.49
  2215.6 18.9 collective-permute-start.48
  2237.6 203.3 %copy-start.1 = (bf16[1,1280,320]{1,2,0:T(8,128)(2,1)S(1)}, bf16[1,1280,320]{1,2,0:T(8,128)(2,1)}, u32[]{:S(2)}) copy-start(bf16[1,1280,320]{1,2,0:T(8,128)(2,1)} %param.14) | copy-start | bytes 2457604
  2390.8 34.7 %collective-permute-start.56 = (f32[16,320]{1,0:T(8,128)S(1)}, f32[16,320]{1,0:T(8,128)S(1)}, u32[]{:S(2)}, u32[]{:S(2)}) collective-permute-start(f32[16,320]{1,0:T(8,128)S(1)} %get-tuple-element.55), channel_id=1, source_target_pairs={{0,3},{1,4},{2,5},{3,6},{4,7},{5,8},{6,9},{7,10},{8,11},{9,12},{10... | collective-permute-start | bytes 61448
  2396.1 36.2 %collective-permute-start.55 = (f32[16,320]{1,0:T(8,128)S(1)}, f32[16,320]{1,0:T(8,128)S(1)}, u32[]{:S(2)}, u32[]{:S(2)}) collective-permute-start(f32[16,320]{1,0:T(8,128)S(1)} %get-tuple-element.55), channel_id=1, source_target_pairs={{0,2},{1,3},{2,4},{3,5},{4,6},{5,7},{6,8},{7,9},{8,10},{9,11},{10,... | collective-permute-start | bytes 61448
  2401.5 32.8 %collective-permute-start.54 = (f32[16,320]{1,0:T(8,128)S(1)}, f32[16,320]{1,0:T(8,128)S(1)}, u32[]{:S(2)}, u32[]{:S(2)}) collective-permute-start(f32[16,320]{1,0:T(8,128)S(1)} %get-tuple-element.55), channel_id=1, source_target_pairs={{0,1},{1,2},{2,3},{3,4},{4,5},{5,6},{6,7},{7,8},{8,9},{9,10},{10,1... | collective-permute-start | bytes 61448
  2405.0 15.8 collective-permute-start.57
  2413.7 24.3 collective-permute-start.52
  2420.8 17.2 collective-permute-start.51
  2425.5 12.5 collective-permute-start.50
  2432.3 5.7 collective-permute-start.53
  (94 other events, 2938.7 us)
Sparse Core Ops, SparseCore 0:
  2224.7 204.9 all-reduce.22
where the time goes:
time: 2450 us
  blocking collectives  1970 us (80%)
  starting transfers between devices  203 us (8%)
  local copies, waits for them, and re-layouts  80.7 us (3%)
  waiting for transfers between devices  61.5 us (3%)
  other arithmetic  55.7 us (2%)
  matrix products  53.3 us (2%)
  between operations  25.5 us (1%)
    psum x5, blocking collectives, per_device(): lax.psum(group_sum(frame_mask * centred * centred), ('frame', 'row'))  627 us
    psum x5, blocking collectives, per_device(): lax.psum((group_sum(normed_grad), group_sum(normed_grad * normed)), ('fra...  605 us
    psum x5, blocking collectives, per_device(): group_mean = lax.psum(group_sum(masked), ('frame', 'row')) / cell_total  583 us
    unnamed x1, blocking collectives  153 us
    ppermute x19, starting transfers between devices, with_halo(): before = lax.ppermute(last, axis, up)  78.6 us
  transfers between devices with their start and end apart: 59, of which 22 were waited for; matrix products, arithmetic and copies ran while one was open for 12% of the time, Pallas kernels for 0%

commit v1 on v0

--- a/solution.py
+++ b/solution.py
@@ -11,6 +11,11 @@
 F_DEV = 2
 CLIPS = 2
 EPSILON = 1e-05
+
+
+def axis_by_axis(x, one, other):
+    half = lax.psum(x, one)
+    return lax.psum(half, other)
 
 
 def with_halo(array, sides, width):
@@ -164,7 +169,7 @@
             act_shape
         ) + pick_row(clip_biases, clip_index)
         masked = hidden * frame_mask
-        group_mean = lax.psum(group_sum(masked), ("frame", "row")) / cell_total
+        group_mean = axis_by_axis(group_sum(masked), "frame", "row") / cell_total
         centred = hidden - spread(group_mean)
         variance = (
             lax.psum(group_sum(frame_mask * centred * centred), ("frame", "row")) / cell_total

time: 2450 us -> 1990 us (0.81)
  blocking collectives: 1970 us -> 1500 us
    psum x5 -> x10, blocking collectives: 583 us -> 206 us  [the longest x5 156 us: axis_by_axis(): half = lax.psum(x, one)]
    psum x5, blocking collectives: 627 us -> 533 us  [per_device(): lax.psum(group_sum(frame_mask * centred * centred), ('frame', 'row'))]
  transfers between devices with their start and end apart: 59 -> 59, of which waited for: 22 -> 22; matrix products, arithmetic and copies ran while one was open for 12% -> 15% of each run, Pallas kernels for 0% -> 0%
where the time goes in v1:
time: 1990 us
  blocking collectives  1500 us (75%)
  starting transfers between devices  207 us (10%)
  local copies, waits for them, and re-layouts  80.3 us (4%)
  waiting for transfers between devices  65.1 us (3%)
  other arithmetic  55.2 us (3%)
  matrix products  53.2 us (3%)
  between operations  25.3 us (1%)
    psum x5, blocking collectives, per_device(): lax.psum((group_sum(normed_grad), group_sum(normed_grad * normed)), ('fra...  605 us
    psum x5, blocking collectives, per_device(): lax.psum(group_sum(frame_mask * centred * centred), ('frame', 'row'))  533 us
    psum x5, blocking collectives, axis_by_axis(): half = lax.psum(x, one)  156 us
    unnamed x1, blocking collectives  155 us
    ppermute x19, starting transfers between devices, with_halo(): before = lax.ppermute(last, axis, up)  74.9 us
    ppermute x19, starting transfers between devices, with_halo(): after = lax.ppermute(leading, axis, down)  58.3 us
    psum x5, blocking collectives, axis_by_axis(): return lax.psum(half, other)  50 us
    unnamed x9, starting transfers between devices  41.2 us
  transfers between devices with their start and end apart: 59, of which 22 were waited for; matrix products, arithmetic and copies ran while one was open for 15% of the time, Pallas kernels for 0%

profile of v1, /device:TPU:80, one launch (start us, length us, event | category | flops | bytes accessed | tf_op | source)
XLA Modules:
  0.0 1985.7 jit_solution(13956408605843367700)
XLA Ops:
  9.6 4.5 collective-permute-start
  20.1 3.6 collective-permute-start.24
  52.9 22.4 %psum.175 = f32[32]{0:T(128)S(1)} all-reduce(f32[32]{0:T(128)S(1)} %reduce_sum.451), channel_id=1, replica_groups=mesh['segment'=4,'frame'=16,'row'=4] {'frame'}, use_global_device_ids=true, to_apply=%region_2.3 | all-reduce | flops 32 | bytes 256 | tf_op jit(solution)/shard_map/psum | solution.py:17
  75.3 9.2 psum.176
  85.5 106.5 %psum.177 = f32[32]{0:T(128)S(1)} all-reduce(f32[32]{0:T(128)S(1)} %reduce_sum.453), channel_id=1, replica_groups=mesh['segment'=4,'frame'=16,'row'=4] {'frame','row'}, use_global_device_ids=true, to_apply=%region_6.7 | all-reduce | flops 32 | bytes 256 | tf_op jit(solution)/shard_map/psum | solution.py:175
  193.6 9.0 collective-permute-start.3
  207.5 3.6 collective-permute-done.2
  213.2 3.3 collective-permute-start.4
  221.1 4.5 collective-permute-start.5
  232.8 32.6 %psum.178 = f32[32]{0:T(128)S(1)} all-reduce(f32[32]{0:T(128)S(1)} %reduce_sum.455), channel_id=1, replica_groups=mesh['segment'=4,'frame'=16,'row'=4] {'frame'}, use_global_device_ids=true, to_apply=%region_9.10 | all-reduce | flops 32 | bytes 256 | tf_op jit(solution)/shard_map/psum | solution.py:17
  265.4 10.1 psum.179
  276.5 106.5 %psum.180 = f32[32]{0:T(128)S(1)} all-reduce(f32[32]{0:T(128)S(1)} %reduce_sum.457), channel_id=1, replica_groups=mesh['segment'=4,'frame'=16,'row'=4] {'frame','row'}, use_global_device_ids=true, to_apply=%region_13.14 | all-reduce | flops 32 | bytes 256 | tf_op jit(solution)/shard_map/psum | solution.py:175
  385.2 7.9 collective-permute-start.8
  403.4 3.2 collective-permute-start.9
  411.0 4.5 collective-permute-start.10
  422.5 33.9 %psum.181 = f32[32]{0:T(128)S(1)} all-reduce(f32[32]{0:T(128)S(1)} %reduce_sum.459), channel_id=1, replica_groups=mesh['segment'=4,'frame'=16,'row'=4] {'frame'}, use_global_device_ids=true, to_apply=%region_16.17 | all-reduce | flops 32 | bytes 256 | tf_op jit(solution)/shard_map/psum | solution.py:17
  456.3 10.1 psum.182
  467.5 106.6 %psum.183 = f32[32]{0:T(128)S(1)} all-reduce(f32[32]{0:T(128)S(1)} %reduce_sum.461), channel_id=1, replica_groups=mesh['segment'=4,'frame'=16,'row'=4] {'frame','row'}, use_global_device_ids=true, to_apply=%region_20.21 | all-reduce | flops 32 | bytes 256 | tf_op jit(solution)/shard_map/psum | solution.py:175
  575.4 8.2 collective-permute-start.13
  593.7 3.2 collective-permute-start.14
  602.2 4.5 collective-permute-start.16
  614.9 34.1 %psum.184 = f32[32]{0:T(128)S(1)} all-reduce(f32[32]{0:T(128)S(1)} %reduce_sum.463), channel_id=1, replica_groups=mesh['segment'=4,'frame'=16,'row'=4] {'frame'}, use_global_device_ids=true, to_apply=%region_23.24 | all-reduce | flops 32 | bytes 256 | tf_op jit(solution)/shard_map/psum | solution.py:17
  649.1 10.3 psum.185
  663.4 106.8 %psum.186 = f32[32]{0:T(128)S(1)} all-reduce(f32[32]{0:T(128)} %reduce_sum.465), channel_id=1, replica_groups=mesh['segment'=4,'frame'=16,'row'=4] {'frame','row'}, use_global_device_ids=true, to_apply=%region_27.28 | all-reduce | flops 32 | bytes 256 | tf_op jit(solution)/shard_map/psum | solution.py:175
  772.3 8.0 collective-permute-start.19
  783.1 5.7 collective-permute-done.18
  790.3 3.2 collective-permute-start.20
  793.6 4.0 collective-permute-done.20
  800.4 4.5 collective-permute-start.22
  812.7 33.2 %psum.187 = f32[32]{0:T(128)S(1)} all-reduce(f32[32]{0:T(128)S(1)} %reduce_sum.467), channel_id=1, replica_groups=mesh['segment'=4,'frame'=16,'row'=4] {'frame'}, use_global_device_ids=true, to_apply=%region_30.31 | all-reduce | flops 32 | bytes 256 | tf_op jit(solution)/shard_map/psum | solution.py:17
  845.9 10.3 psum.188
  857.6 106.5 %psum.189 = f32[32]{0:T(128)S(1)} all-reduce(f32[32]{0:T(128)S(1)} %reduce_sum.469), channel_id=1, replica_groups=mesh['segment'=4,'frame'=16,'row'=4] {'frame','row'}, use_global_device_ids=true, to_apply=%region_34.35 | all-reduce | flops 32 | bytes 256 | tf_op jit(solution)/shard_map/psum | solution.py:175
  969.9 125.0 %all-reduce.19 = (f32[32]{0:T(128)S(1)}, f32[32]{0:T(128)S(1)}) all-reduce(f32[32]{0:T(128)S(1)} %reduce_sum.473, f32[32]{0:T(128)S(1)} %reduce_sum.471), channel_id=1, replica_groups=mesh['segment'=4,'frame'=16,'row'=4] {'frame','row'}, use_global_device_ids=true, to_apply=%region_40.41 | all-reduce | flops 64 | bytes 512 | tf_op jit(solution)/shard_map/psum | solution.py:222
  1098.2 4.6 collective-permute-start.26
  1109.6 3.9 collective-permute-start.28
  1116.5 4.2 collective-permute-start.30
  1124.4 9.5 collective-permute-done.29
  1137.1 119.3 %all-reduce.18 = (f32[32]{0:T(128)S(1)}, f32[32]{0:T(128)S(1)}) all-reduce(f32[32]{0:T(128)S(1)} %reduce_sum.477, f32[32]{0:T(128)S(1)} %reduce_sum.475), channel_id=1, replica_groups=mesh['segment'=4,'frame'=16,'row'=4] {'frame','row'}, use_global_device_ids=true, to_apply=%region_46.47 | all-reduce | flops 64 | bytes 512 | tf_op jit(solution)/shard_map/psum | solution.py:222
  1259.7 4.5 collective-permute-start.31
  1271.7 4.0 collective-permute-start.33
  1279.0 4.2 collective-permute-start.35
  1286.5 10.0 collective-permute-done.34
  1299.7 118.0 %all-reduce.17 = (f32[32]{0:T(128)S(1)}, f32[32]{0:T(128)S(1)}) all-reduce(f32[32]{0:T(128)S(1)} %reduce_sum.481, f32[32]{0:T(128)S(1)} %reduce_sum.479), channel_id=1, replica_groups=mesh['segment'=4,'frame'=16,'row'=4] {'frame','row'}, use_global_device_ids=true, to_apply=%region_52.53 | all-reduce | flops 64 | bytes 512 | tf_op jit(solution)/shard_map/psum | solution.py:222
  1420.4 4.5 collective-permute-start.36
  1432.6 4.1 collective-permute-start.38
  1441.9 4.7 collective-permute-start.41
  1465.8 125.6 %all-reduce.16 = (f32[32]{0:T(128)S(1)}, f32[32]{0:T(128)S(1)}) all-reduce(f32[32]{0:T(128)S(1)} %reduce_sum.485, f32[32]{0:T(128)S(1)} %reduce_sum.483), channel_id=1, replica_groups=mesh['segment'=4,'frame'=16,'row'=4] {'frame','row'}, use_global_device_ids=true, to_apply=%region_58.59 | all-reduce | flops 64 | bytes 512 | tf_op jit(solution)/shard_map/psum | solution.py:222
  1593.3 4.8 collective-permute-start.42
  1598.1 3.8 convolution_bitcast_fusion.3
  1610.3 2.9 convolution_bitcast_fusion.2
  1615.1 4.8 collective-permute-start.47
  1621.9 2.9 convolution_bitcast_fusion.1
  1624.9 7.7 collective-permute-done.46
  1633.5 117.5 %all-reduce.15 = (f32[32]{0:T(128)S(1)}, f32[32]{0:T(128)S(1)}, f32[320]{0:T(512)S(1)}) all-reduce(f32[32]{0:T(128)S(1)} %reduce_sum.489, f32[32]{0:T(128)S(1)} %reduce_sum.487, f32[320]{0:T(512)S(1)} %select_add_fusion.2), channel_id=1, replica_groups=mesh['segment'=4,'frame'=16,'row'=4] {'frame','row'}, use_global_device_ids=true, to_apply=%region_64.65 | all-reduce | flops 384 | bytes 3072 | tf_op jit(solution)/shard_map/psum | solution.py:222
  1753.5 6.3 collective-permute-start.48
  1764.8 7.5 select_add_fusion
  1775.4 154.9 %fusion.209 = (f32[48,320]{1,0:T(8,128)S(1)}, f32[16,320]{1,0:T(8,128)S(1)}) fusion(f32[2880,320]{1,0:T(8,128)} %select_add_fusion, f32[960,320]{1,0:T(8,128)S(1)} %fusion.2), kind=kCustom, calls=%all-reduce-scatter.2 | all-reduce-scatter fusion | flops 1310722 | bytes 4998144
  1930.4 4.9 collective-permute-start.56
  1935.3 3.6 collective-permute-start.55
  1938.9 3.8 collective-permute-start.54
  1942.7 8.0 collective-permute-start.57
  1951.3 6.6 collective-permute-start.52
  1957.9 5.6 collective-permute-start.51
  1963.5 6.8 collective-permute-start.50
  (589 shorter events, 237.1 us)
Async XLA Ops:
  7.2 1970.3 %all-reduce.23.cloned.1.call-start = ((), (), s32[]{:S(2)}) async-start(), calls=%async_computation | async-start | bytes 3932160
  8.3 41.8 %collective-permute-start.1 = (bf16[2,1,24,320]{3,2,1,0:T(8,128)(2,1)S(1)}, bf16[2,1,24,320]{3,2,1,0:T(8,128)(2,1)S(1)}, u32[]{:S(2)}, u32[]{:S(2)}) collective-permute-start(bf16[2,1,24,320]{3,2,1,0:T(8,128)(2,1)S(1)} %get-tuple-element.260), channel_id=1, source_target_pairs={{1,0},{2,1},{3,2},{5,4},{6,5},{7,6},{9,8},{10,9},{11,10},{13,12},{... | collective-permute-start | bytes 92168 | tf_op jit(solution)/shard_map/ppermute | solution.py:29
  9.6 40.5 %collective-permute-start = (bf16[2,1,24,320]{3,2,1,0:T(8,128)(2,1)S(1)}, bf16[2,1,24,320]{3,2,1,0:T(8,128)(2,1)S(1)}, u32[]{:S(2)}, u32[]{:S(2)}) collective-permute-start(bf16[2,1,24,320]{3,2,1,0:T(8,128)(2,1)S(1)} %get-tuple-element.259), channel_id=1, source_target_pairs={{0,1},{1,2},{2,3},{4,5},{5,6},{6,7},{8,9},{9,10},{10,11},{12,13},{... | collective-permute-start | bytes 92168 | tf_op jit(solution)/shard_map/ppermute | solution.py:28
  18.2 948.4 %collective-permute-start.25 = (bf16[1,2,24,320]{3,2,1,0:T(8,128)(2,1)}, bf16[1,2,24,320]{3,2,1,0:T(8,128)(2,1)}, u32[]{:S(2)}, u32[]{:S(2)}) collective-permute-start(bf16[1,2,24,320]{3,2,1,0:T(8,128)(2,1)} %get-tuple-element.234), channel_id=1, source_target_pairs={{0,4},{4,8},{8,12},{12,16},{16,20},{20,24},{24,28},{28,32},{32,36}... | collective-permute-start | bytes 92168 | tf_op jit(solution)/shard_map/ppermute | solution.py:28
  20.1 946.5 %collective-permute-start.24 = (bf16[1,2,24,320]{3,2,1,0:T(8,128)(2,1)}, bf16[1,2,24,320]{3,2,1,0:T(8,128)(2,1)}, u32[]{:S(2)}, u32[]{:S(2)}) collective-permute-start(bf16[1,2,24,320]{3,2,1,0:T(8,128)(2,1)} %get-tuple-element.233), channel_id=1, source_target_pairs={{4,0},{8,4},{12,8},{16,12},{20,16},{24,20},{28,24},{32,28},{36,32}... | collective-permute-start | bytes 92168 | tf_op jit(solution)/shard_map/ppermute | solution.py:29
  26.9 547.9 %copy-start.74 = (f32[2]{0:T(128)}, f32[2]{0:T(128)S(1)}, u32[]{:S(2)}) copy-start(f32[2]{0:T(128)S(1)} %compare_convert_fusion.7) | copy-start | bytes 28
  193.6 13.9 collective-permute-start.3
  202.6 8.5 collective-permute-start.2
  213.2 6.6 collective-permute-start.4
  217.2 380.4 %collective-permute-start.15 = (bf16[2,2,24,320]{3,2,1,0:T(8,128)(2,1)}, bf16[2,2,24,320]{3,2,1,0:T(8,128)(2,1)}, u32[]{:S(2)}, u32[]{:S(2)}) collective-permute-start(bf16[2,2,24,320]{3,2,1,0:T(8,128)(2,1)} %fusion.16), channel_id=1, source_target_pairs={{0,192},{1,193},{2,194},{3,195},{4,196},{5,197},{6,198},{7,199},{8... | collective-permute-start | bytes 184328 | tf_op jit(solution)/shard_map/ppermute | solution.py:37
  219.8 6.8 collective-permute-start.6
  221.1 6.4 collective-permute-start.5
  385.2 13.9 collective-permute-start.8
  393.1 8.8 collective-permute-start.7
  403.4 6.2 collective-permute-start.9
  409.7 6.7 collective-permute-start.11
  411.0 6.2 collective-permute-start.10
  575.4 13.6 collective-permute-start.13
  583.7 8.5 collective-permute-start.12
  589.0 204.6 %collective-permute-start.21 = (bf16[2,2,24,320]{3,2,1,0:T(8,128)(2,1)}, bf16[2,2,24,320]{3,2,1,0:T(8,128)(2,1)}, u32[]{:S(2)}, u32[]{:S(2)}) collective-permute-start(bf16[2,2,24,320]{3,2,1,0:T(8,128)(2,1)} %copy-done.98), channel_id=1, source_target_pairs={{0,192},{1,193},{2,194},{3,195},{4,196},{5,197},{6,198},{7,199},{8... | collective-permute-start | bytes 184328 | tf_op jit(solution)/shard_map/ppermute | solution.py:37
  593.7 6.2 collective-permute-start.14
  600.8 192.7 %copy-start.9 = (bf16[2,2,24,320]{3,2,1,0:T(8,128)(2,1)}, bf16[2,2,24,320]{3,2,1,0:T(8,128)(2,1)S(1)}, u32[]{:S(2)}) copy-start(bf16[2,2,24,320]{3,2,1,0:T(8,128)(2,1)S(1)} %fusion.136) | copy-start | bytes 184324
  600.9 6.6 collective-permute-start.17
  602.2 6.2 collective-permute-start.16
  611.7 170.5 %copy-start.42 = (bf16[1,2,2,24,320]{4,3,2,1,0:T(8,128)(2,1)S(1)}, bf16[1,2,2,24,320]{4,3,2,1,0:T(8,128)(2,1)}, u32[]{:S(2)}) copy-start(bf16[1,2,2,24,320]{4,3,2,1,0:T(8,128)(2,1)} %fusion.289) | copy-start | bytes 184324
  772.3 10.8 collective-permute-start.19
  780.3 8.5 collective-permute-start.18
  790.3 7.3 collective-permute-start.20
  799.1 7.2 collective-permute-start.23
  800.4 6.2 collective-permute-start.22
  810.1 156.6 %copy-start.27 = (bf16[2,2,24,320]{3,2,1,0:T(8,128)(2,1)S(1)}, bf16[2,2,24,320]{3,2,1,0:T(8,128)(2,1)}, u32[]{:S(2)}) copy-start(bf16[2,2,24,320]{3,2,1,0:T(8,128)(2,1)} %copy-done.26) | copy-start | bytes 184324
  1096.9 7.0 collective-permute-start.27
  1098.2 6.2 collective-permute-start.26
  1109.6 6.2 collective-permute-start.28
  1116.5 7.9 collective-permute-start.30
  1120.8 13.2 collective-permute-start.29
  1258.4 6.8 collective-permute-start.32
  1259.7 6.2 collective-permute-start.31
  1271.7 6.6 collective-permute-start.33
  1279.0 7.4 collective-permute-start.35
  1283.2 13.2 collective-permute-start.34
  1419.1 8.3 collective-permute-start.37
  1420.4 7.0 collective-permute-start.36
  1426.1 11.7 collective-permute-start.39
  1432.6 7.6 collective-permute-start.38
  1441.9 21.9 %collective-permute-start.41 = (bf16[1,2,24,320]{3,2,1,0:T(8,128)(2,1)}, bf16[1,2,24,320]{3,2,1,0:T(8,128)(2,1)}, u32[]{:S(2)}, u32[]{:S(2)}) collective-permute-start(bf16[1,2,24,320]{3,2,1,0:T(8,128)(2,1)} %get-tuple-element.214), channel_id=1, source_target_pairs={{0,4},{4,8},{8,12},{12,16},{16,20},{20,24},{24,28},{28,32},{32,36}... | collective-permute-start | bytes 92168 | tf_op jit(solution)/shard_map/ppermute | solution.py:28
  1446.6 17.2 collective-permute-start.40
  1592.0 11.3 collective-permute-start.43
  1593.3 10.0 collective-permute-start.42
  1601.9 11.2 collective-permute-start.45
  1607.7 6.4 collective-permute-start.44
  1615.1 9.8 collective-permute-start.47
  1619.8 12.8 collective-permute-start.46
  1751.5 20.8 %collective-permute-start.49 = (bf16[1,2,24,320]{3,2,1,0:T(8,128)(2,1)S(1)}, bf16[1,2,24,320]{3,2,1,0:T(8,128)(2,1)S(1)}, u32[]{:S(2)}, u32[]{:S(2)}) collective-permute-start(bf16[1,2,24,320]{3,2,1,0:T(8,128)(2,1)S(1)} %get-tuple-element.206), channel_id=1, source_target_pairs={{4,0},{8,4},{12,8},{16,12},{20,16},{24,20},{28,24},{32,28},{36,32}... | collective-permute-start | bytes 92168 | tf_op jit(solution)/shard_map/ppermute | solution.py:29
  1753.5 18.8 collective-permute-start.48
  1775.4 203.5 %copy-start.1 = (bf16[1,1280,320]{1,2,0:T(8,128)(2,1)S(1)}, bf16[1,1280,320]{1,2,0:T(8,128)(2,1)}, u32[]{:S(2)}) copy-start(bf16[1,1280,320]{1,2,0:T(8,128)(2,1)} %param.14) | copy-start | bytes 2457604
  1930.4 33.1 %collective-permute-start.56 = (f32[16,320]{1,0:T(8,128)S(1)}, f32[16,320]{1,0:T(8,128)S(1)}, u32[]{:S(2)}, u32[]{:S(2)}) collective-permute-start(f32[16,320]{1,0:T(8,128)S(1)} %get-tuple-element.55), channel_id=1, source_target_pairs={{0,3},{1,4},{2,5},{3,6},{4,7},{5,8},{6,9},{7,10},{8,11},{9,12},{10... | collective-permute-start | bytes 61448
  1935.3 35.0 %collective-permute-start.55 = (f32[16,320]{1,0:T(8,128)S(1)}, f32[16,320]{1,0:T(8,128)S(1)}, u32[]{:S(2)}, u32[]{:S(2)}) collective-permute-start(f32[16,320]{1,0:T(8,128)S(1)} %get-tuple-element.55), channel_id=1, source_target_pairs={{0,2},{1,3},{2,4},{3,5},{4,6},{5,7},{6,8},{7,9},{8,10},{9,11},{10,... | collective-permute-start | bytes 61448
  1938.9 33.3 %collective-permute-start.54 = (f32[16,320]{1,0:T(8,128)S(1)}, f32[16,320]{1,0:T(8,128)S(1)}, u32[]{:S(2)}, u32[]{:S(2)}) collective-permute-start(f32[16,320]{1,0:T(8,128)S(1)} %get-tuple-element.55), channel_id=1, source_target_pairs={{0,1},{1,2},{2,3},{3,4},{4,5},{5,6},{6,7},{7,8},{8,9},{9,10},{10,1... | collective-permute-start | bytes 61448
  1942.7 15.2 collective-permute-start.57
  1951.3 24.7 %collective-permute-start.52 = (f32[48,320]{1,0:T(8,128)S(1)}, f32[48,320]{1,0:T(8,128)S(1)}, u32[]{:S(2)}, u32[]{:S(2)}) collective-permute-start(f32[48,320]{1,0:T(8,128)S(1)} %get-tuple-element.54), channel_id=1, source_target_pairs={{0,3},{1,4},{2,5},{3,6},{4,7},{5,8},{6,9},{7,10},{8,11},{9,12},{10... | collective-permute-start | bytes 184328
  1957.9 18.1 collective-permute-start.51
  1963.5 12.5 collective-permute-start.50
  1970.3 5.7 collective-permute-start.53
  (94 other events, 2886.7 us)
Sparse Core Ops, SparseCore 0:
  1762.5 205.2 all-reduce.22
